TPU v7x, 128 devices: a whole 4x4x4 slice. The times are simulated.
128 devices in a mesh: st: 4 (over y_hi, core), col: 32 (over x, z, y_lo).
Axes of the slice: x: 4, y: 4 (y_hi: 2, y_lo: 2; y = y_hi * 2 + y_lo), z: 4, core: 2. Of those that a mesh axis runs over, the one named last changes fastest.
Arguments:
- forcing: bfloat16 [8, 2048, 8192], P('st', None, 'col'), may hold values from -6 to 6
- operator_rows: bfloat16 [8, 2048, 2048], P('st', 'col'), may hold values from -0.078125 to 0.078125
- counts: int32 [8], P('st'), may hold values from 1 to 3, as said below
- owner_map: int32 [8, 32], P('st'), may hold values from 0 to 31, each once within a row
Outputs:
- adjoint: bfloat16 [8, 2048, 8192], P('st', None, 'col')
Inputs may be any that keep to these rules, and one draw needn't show every extreme that they name: `counts`: some station has exactly 3 terms. `owner_map`: each station's row is a permutation of the row blocks.
All inputs are finite; a program needn't handle non-finite values.
Results may differ from a plain program's by a relative error of at most 0.015.
Values may be sent and summed in bfloat16 or wider, within the bound.
No kernel may reach another device: no remote copies, remote signals or barrier semaphores. Data moves between devices by JAX's collectives and lax.ppermute only.
A program may use at most 128 MiB of HBM per device.

v0:
```python
import jax
import jax.numpy as jnp
from jax import lax
from jax.sharding import PartitionSpec as P


def from_behind(x, axis, by):
    peers = lax.axis_size(axis)
    pairs = [(i, i + by) for i in range(peers) if 0 <= i + by < peers]
    return lax.ppermute(x, axis, pairs)


def reorder(stored, mapping):
    owners = mapping.shape[0]
    blocks = stored.reshape(owners, stored.shape[0] // owners, stored.shape[1])
    slots = jnp.arange(owners, dtype=jnp.int32)
    inverse = jnp.sum(jnp.where(mapping[None, :] == slots[:, None], slots[None, :], 0), axis=1)
    return jnp.take(blocks, inverse, axis=0).reshape(stored.shape)


def advance(matrix, incoming, force, count):
    start = (incoming.astype(jnp.float32) + force.astype(jnp.float32)).astype(jnp.bfloat16)

    def power(index, carry):
        phi, total = carry
        phi = jnp.dot(matrix, phi, preferred_element_type=jnp.float32).astype(jnp.bfloat16)
        return (phi, total + phi.astype(jnp.float32))

    phi, total = lax.fori_loop(0, count, power, (start, start.astype(jnp.float32)))
    return (0.7 * total).astype(jnp.bfloat16)


def send_down(state):
    return from_behind(state, "st", -1)


def shards(forcing, operator_rows, counts, owner_map):
    upper = lax.all_gather(operator_rows[1], "col", axis=0, tiled=True)
    lower = lax.all_gather(operator_rows[0], "col", axis=0, tiled=True)
    upper = reorder(upper, owner_map[1])
    lower = reorder(lower, owner_map[0])
    sections = lax.axis_size("st")
    place = lax.axis_index("st")
    width = forcing.shape[2]
    pieces = 1
    span = width // pieces
    result = jnp.zeros_like(forcing)
    outgoing = jnp.zeros((forcing.shape[1], span), jnp.bfloat16)
    for turn in range(sections + pieces - 1):
        received = send_down(outgoing)
        block = turn - (sections - 1 - place)
        valid = jnp.logical_and(block >= 0, block < pieces)

        def work(operands):
            incoming, current = operands
            force_upper = forcing[1]
            force_lower = forcing[0]
            state_upper = advance(upper, incoming, force_upper, counts[1])
            state_lower = advance(lower, state_upper, force_lower, counts[0])
            current = jnp.stack([state_lower, state_upper])
            return (state_lower, current)

        def keep(operands):
            return (operands[0], operands[1])

        outgoing, result = lax.cond(valid, work, keep, (received, result))
    return result


def solution(mesh):
    in_specs = (P("st", None, "col"), P("st", "col", None), P("st"), P("st", None))
    out_specs = P("st", None, "col")
    return jax.shard_map(shards, mesh=mesh, in_specs=in_specs, out_specs=out_specs, check_vma=False)
```

profile of v0, /device:TPU:0, one launch (start us, length us, event | category | flops | bytes accessed | tf_op | source)
XLA Modules:
  0.0 660.6 jit_solution(188656802177164767)
XLA Ops:
  6.5 1.9 fusion.33
  11.8 188.9 %all-gather.7.cloned.1.call-done = bf16[1,2048,2048]{2,1,0:T(8,128)(2,1)} async-done(((bf16[1,64,2048]{2,1,0:T(8,128)(2,1)}), bf16[1,2048,2048]{2,1,0:T(8,128)(2,1)}) %all-gather.7.cloned.1.call-update) | async-done | bytes 8388624 | tf_op jit(solution)/shard_map/all_gather | solution.py:39
  200.7 8.5 %gather_fusion.1 = bf16[32,64,2048]{2,1,0:T(8,128)(2,1)} fusion(bf16[32,64,2048]{2,1,0:T(8,128)(2,1)} %bitcast.120, s32[1024]{0:T(1024)S(1)} %pad_clamp_fusion), kind=kCustom, calls=%fused_computation.1.clone | custom fusion | bytes 16777344 | tf_op jit(solution)/shard_map/jit(_take)/gather | solution.py:18
  209.2 7.6 %broadcast_select_fusion = bf16[32,64,2048]{2,1,0:T(8,128)(2,1)} fusion(bf16[32,64,2048]{2,1,0:T(8,128)(2,1)} %gather_fusion.1, pred[32]{0:T(512)(128)(4,1)S(1)} %compare_and_fusion), kind=kLoop, calls=%fused_computation.51 | loop fusion | flops 4194304 | bytes 16777248 | tf_op jit(solution)/shard_map/jit(_take)/select_n | solution.py:18
  216.8 180.8 %all-gather.5.cloned.1.call-done = bf16[1,2048,2048]{2,1,0:T(8,128)(2,1)} async-done(((bf16[1,64,2048]{2,1,0:T(8,128)(2,1)}), bf16[1,2048,2048]{2,1,0:T(8,128)(2,1)}) %all-gather.5.cloned.1.call-update) | async-done | bytes 8388624 | tf_op jit(solution)/shard_map/all_gather | solution.py:38
  397.6 8.5 %gather_fusion = bf16[32,64,2048]{2,1,0:T(8,128)(2,1)} fusion(bf16[32,64,2048]{2,1,0:T(8,128)(2,1)} %bitcast.121, s32[1024]{0:T(1024)S(1)} %pad_clamp_fusion.1), kind=kCustom, calls=%fused_computation.clone | custom fusion | bytes 16777344 | tf_op jit(solution)/shard_map/jit(_take)/gather | solution.py:18
  406.1 7.7 %broadcast_select_fusion.1 = bf16[32,64,2048]{2,1,0:T(8,128)(2,1)} fusion(bf16[32,64,2048]{2,1,0:T(8,128)(2,1)} %gather_fusion, pred[32]{0:T(512)(128)(4,1)S(1)} %compare_and_fusion.1), kind=kLoop, calls=%fused_computation.52 | loop fusion | flops 4194304 | bytes 16777248 | tf_op jit(solution)/shard_map/jit(_take)/select_n | solution.py:18
  413.8 1.5 conditional.4
  413.8 1.5 broadcast_in_dim.32
  416.6 3.4 collective-permute-done.1
  419.9 1.3 collective-permute-start.2
  421.2 15.3 %collective-permute-done.2 = bf16[2048,256]{1,0:T(8,128)(2,1)S(1)} collective-permute-done((bf16[2048,256]{1,0:T(8,128)(2,1)}, bf16[2048,256]{1,0:T(8,128)(2,1)S(1)}, u32[]{:S(2)}, u32[]{:S(2)}) %collective-permute-start.2) | collective-permute-done | bytes 1048608 | tf_op jit(solution)/shard_map/ppermute | solution.py:10
  438.8 164.1 %collective-permute-done.3 = bf16[2048,256]{1,0:T(8,128)(2,1)S(1)} collective-permute-done((bf16[2048,256]{1,0:T(8,128)(2,1)}, bf16[2048,256]{1,0:T(8,128)(2,1)S(1)}, u32[]{:S(2)}, u32[]{:S(2)}) %collective-permute-start.3) | collective-permute-done | bytes 1048608 | tf_op jit(solution)/shard_map/ppermute | solution.py:10
  602.9 50.8 %conditional.7 = (bf16[2,2048,256]{2,1,0:T(8,128)(2,1)}) conditional(s32[]{:T(128)} %convert_element_type.204, bf16[2,2048,256]{2,1,0:T(8,128)(2,1)} %get-tuple-element.316, (bf16[2048,256]{1,0:T(8,128)(2,1)S(1)}, bf16[2,2048,256]{2,1,0:T(8,128)(2,1)S(1)}, s32[2]{0:T(128)S(1)}, bf16[2048,2048]{1,0:T(8,128)(2,1)}, ...), branch_computations={%region_20.22_spmd, %region_21.27_spmd} | conditional | flops 4306501632 | bytes 95420856 | solution.py:66
  604.0 2.8 fusion.27
  606.8 10.3 %while.88 = (s32[]{:T(128)}, bf16[2048,256]{1,0:T(8,128)(2,1)S(1)}, f32[2048,256]{1,0:T(8,128)}, s32[]{:T(128)}, bf16[2048,2048]{1,0:T(8,128)(2,1)}, /*index=5*/s32[]{:T(128)}) while((s32[]{:T(128)}, bf16[2048,256]{1,0:T(8,128)(2,1)S(1)}, f32[2048,256]{1,0:T(8,128)}, s32[]{:T(128)}, bf16[2048,2048]{1,0:T(8,128)(2,1)}, ...), condition=%wide.region_23.24_spmd, body=%wide.region_22.23_spmd.sunk | while | flops 2149056512 | bytes 33554556 | solution.py:29
  607.5 1.5 copy-done.18
  609.0 6.0 convert_add_fusion.24
  615.0 1.3 copy-done.19
  617.0 3.7 fusion.25
  620.8 29.5 %while.89 = (s32[]{:T(128)}, bf16[2048,256]{1,0:T(8,128)(2,1)S(1)}, f32[2048,256]{1,0:T(8,128)}, s32[]{:T(128)}, bf16[2048,2048]{1,0:T(8,128)(2,1)}, /*index=5*/s32[]{:T(128)}) while((s32[]{:T(128)}, bf16[2048,256]{1,0:T(8,128)(2,1)S(1)}, f32[2048,256]{1,0:T(8,128)}, s32[]{:T(128)}, bf16[2048,2048]{1,0:T(8,128)(2,1)}, ...), condition=%wide.region_25.26_spmd, body=%wide.region_24.25_spmd.sunk | while | flops 2149056512 | bytes 33554556 | solution.py:29
  621.8 1.5 copy-done.10
  623.3 6.0 convert_add_fusion.25
  629.3 1.3 copy-done.11
  631.3 1.5 copy-done.10
  632.8 6.0 convert_add_fusion.25
  638.8 1.3 copy-done.11
  640.8 1.5 copy-done.10
  642.4 6.0 convert_add_fusion.25
  648.3 1.3 copy-done.11
  650.3 1.9 fusion.11
  652.2 1.5 pad_maximum_fusion.3
  (45 shorter events, 8.3 us)
Async XLA Ops:
  6.5 5.0 copy-start.29
  6.5 194.2 %all-gather.7.cloned.1.call-start = ((), (), s32[]{:S(2)}) async-start(), calls=%async_computation.1 | async-start | bytes 8650752 | tf_op jit(solution)/shard_map/all_gather | solution.py:39
  8.4 389.2 %all-gather.5.cloned.1.call-start = ((), (), s32[]{:S(2)}) async-start(), calls=%async_computation | async-start | bytes 8650752 | tf_op jit(solution)/shard_map/all_gather | solution.py:38
  10.2 403.6 %collective-permute-start = (bf16[2048,256]{1,0:T(8,128)(2,1)}, bf16[2048,256]{1,0:T(8,128)(2,1)S(1)}, u32[]{:S(2)}, u32[]{:S(2)}) collective-permute-start(bf16[2048,256]{1,0:T(8,128)(2,1)} %broadcast_in_dim.37), channel_id=1, source_target_pairs={{32,0},{64,32},{96,64},{33,1},{65,33},{97,65},{34,2},{66,34},{98,6... | collective-permute-start | bytes 3145736 | tf_op jit(solution)/shard_map/ppermute | solution.py:10
  406.1 7.7 %copy-start = (bf16[2,2048,256]{2,1,0:T(8,128)(2,1)S(1)}, bf16[2,2048,256]{2,1,0:T(8,128)(2,1)}, u32[]{:S(2)}) copy-start(bf16[2,2048,256]{2,1,0:T(8,128)(2,1)} %param.30) | copy-start | bytes 6291460
  406.1 7.7 %copy-start.28 = (s32[2]{0:T(128)S(1)}, s32[2]{0:T(128)}, u32[]{:S(2)}) copy-start(s32[2]{0:T(128)} %param.32) | copy-start | bytes 28
  415.3 4.7 collective-permute-start.1
  419.9 16.6 %collective-permute-start.2 = (bf16[2048,256]{1,0:T(8,128)(2,1)}, bf16[2048,256]{1,0:T(8,128)(2,1)S(1)}, u32[]{:S(2)}, u32[]{:S(2)}) collective-permute-start(bf16[2048,256]{1,0:T(8,128)(2,1)} %get-tuple-element.314), channel_id=1, source_target_pairs={{32,0},{64,32},{96,64},{33,1},{65,33},{97,65},{34,2},{66,34},{98,6... | collective-permute-start | bytes 3145736 | tf_op jit(solution)/shard_map/ppermute | solution.py:10
  436.5 1.0 copy-start.27
  437.5 165.4 %collective-permute-start.3 = (bf16[2048,256]{1,0:T(8,128)(2,1)}, bf16[2048,256]{1,0:T(8,128)(2,1)S(1)}, u32[]{:S(2)}, u32[]{:S(2)}) collective-permute-start(bf16[2048,256]{1,0:T(8,128)(2,1)} %copy-done.27), channel_id=1, source_target_pairs={{32,0},{64,32},{96,64},{33,1},{65,33},{97,65},{34,2},{66,34},{98,6... | collective-permute-start | bytes 3145736 | tf_op jit(solution)/shard_map/ppermute | solution.py:10
  602.9 1.0 copy-start.25
  607.4 1.6 copy-start.18
  615.0 1.3 copy-start.19
  621.7 1.6 copy-start.10
  629.2 1.3 copy-start.11
  631.2 1.6 copy-start.10
  638.8 1.3 copy-start.11
  640.8 1.6 copy-start.10
  648.3 1.3 copy-start.11
  650.3 1.9 copy-start.23
Sparse Core Ops, SparseCore 0:
  9.0 191.6 all-gather.6
  202.4 195.2 all-gather.4
where the time goes:
time: 661 us
  waiting for transfers between devices  553 us (84%)
  local copies, waits for them, and re-layouts  35 us (5%)
  other arithmetic  25.5 us (4%)
  matrix products  23.9 us (4%)
  between operations  13.5 us (2%)
    all_gather x1, waiting for transfers between devices, shards(): lower = lax.all_gather(operator_rows[0], 'col', axis=0, tiled=True)  189 us
    ppermute x4, waiting for transfers between devices, from_behind(): return lax.ppermute(x, axis, pairs)  183 us
    all_gather x1, waiting for transfers between devices, shards(): upper = lax.all_gather(operator_rows[1], 'col', axis=0, tiled=True)  181 us
    dot_general x4, matrix products, power(): jnp.dot(matrix, phi, preferred_element_type=jnp.float32)  23.9 us
    gather x2, local copies, waits for them, and re-layouts, reorder(): return jnp.take(blocks, inverse, axis=0).reshape(stored.shape)  17 us
    select_n x4, other arithmetic, reorder(): return jnp.take(blocks, inverse, axis=0).reshape(stored.shape)  15.3 us
  transfers between devices with their start and end apart: 6, of which 5 were waited for; matrix products, arithmetic and copies ran while one was open for 5% of the time, Pallas kernels for 0%

commit v1 on v0

--- a/solution.py
+++ b/solution.py
@@ -35,7 +35,9 @@
 
 
 def shards(forcing, operator_rows, counts, owner_map):
-    upper = lax.all_gather(operator_rows[1], "col", axis=0, tiled=True)
+    upper = jnp.concatenate(
+        lax.all_to_all(jnp.stack([operator_rows[1]] * lax.axis_size("col")), "col", 0, 0), axis=0
+    )
     lower = lax.all_gather(operator_rows[0], "col", axis=0, tiled=True)
     upper = reorder(upper, owner_map[1])
     lower = reorder(lower, owner_map[0])

time: 661 us -> 585 us (0.89)
  waiting for transfers between devices: 553 us -> 459 us
  starting transfers between devices: 5.16 us -> 14.9 us
    all_gather x1 -> x0, waiting for transfers between devices: 181 us -> none  [shards(): upper = lax.all_gather(operator_rows[1], 'col', axis=0, tiled=True)]
    all_to_all x0 -> x1, waiting for transfers between devices: none -> 124 us  [shards(): lax.all_to_all(jnp.stack([operator_rows[1]] * lax.axis_size('col')), 'col...]
    all_gather x1, waiting for transfers between devices: 189 us -> 139 us  [shards(): lower = lax.all_gather(operator_rows[0], 'col', axis=0, tiled=True)]
    ppermute x4, waiting for transfers between devices: 183 us -> 196 us  [from_behind(): return lax.ppermute(x, axis, pairs)]
    all_to_all x0 -> x1, starting transfers between devices: none -> 9.55 us  [shards(): lax.all_to_all(jnp.stack([operator_rows[1]] * lax.axis_size('col')), 'col...]
  transfers between devices with their start and end apart: 6 -> 6, of which waited for: 5 -> 5; matrix products, arithmetic and copies ran while one was open for 5% -> 7% of each run, Pallas kernels for 0% -> 0%
where the time goes in v1:
time: 585 us; the launch traced here: 580 us
  waiting for transfers between devices  459 us (78%)
  local copies, waits for them, and re-layouts  39.3 us (7%)
  other arithmetic  25.5 us (4%)
  matrix products  23.9 us (4%)
  starting transfers between devices  14.9 us (3%)
  between operations  13.5 us (2%)
    ppermute x4, waiting for transfers between devices, from_behind(): return lax.ppermute(x, axis, pairs)  196 us
    all_gather x1, waiting for transfers between devices, shards(): lower = lax.all_gather(operator_rows[0], 'col', axis=0, tiled=True)  139 us
    all_to_all x1, waiting for transfers between devices, shards(): lax.all_to_all(jnp.stack([operator_rows[1]] * lax.axis_size('col')), 'col...  124 us
    dot_general x4, matrix products, power(): jnp.dot(matrix, phi, preferred_element_type=jnp.float32)  23.9 us
    gather x2, local copies, waits for them, and re-layouts, reorder(): return jnp.take(blocks, inverse, axis=0).reshape(stored.shape)  17 us
    select_n x4, other arithmetic, reorder(): return jnp.take(blocks, inverse, axis=0).reshape(stored.shape)  15.3 us
  transfers between devices with their start and end apart: 6, of which 5 were waited for; matrix products, arithmetic and copies ran while one was open for 7% of the time, Pallas kernels for 0%

profile of v1, /device:TPU:0, one launch (start us, length us, event | category | flops | bytes accessed | tf_op | source)
XLA Modules:
  0.0 580.0 jit_solution(14507644566514386617)
XLA Ops:
  6.5 1.8 fusion.33
  8.3 4.4 stack.39
  12.7 9.5 %all-to-all-start = ((bf16[32,64,2048]{2,1,0:T(8,128)(2,1)}), bf16[32,64,2048]{2,1,0:T(8,128)(2,1)}, u32[]{:S(2)}, u32[]{:S(2)}) async-start(bf16[32,64,2048]{2,1,0:T(8,128)(2,1)} %stack.39), calls=%async_computation | async-start | bytes 16777216 | tf_op jit(solution)/shard_map/all_to_all | solution.py:39
  24.9 124.1 %all-to-all-done = bf16[32,64,2048]{2,1,0:T(8,128)(2,1)} async-done(((bf16[32,64,2048]{2,1,0:T(8,128)(2,1)}), bf16[32,64,2048]{2,1,0:T(8,128)(2,1)}, u32[]{:S(2)}, u32[]{:S(2)}) %all-to-all-start) | async-done | bytes 8388640 | tf_op jit(solution)/shard_map/all_to_all | solution.py:39
  149.0 8.5 %gather_fusion = bf16[32,64,2048]{2,1,0:T(8,128)(2,1)} fusion(bf16[32,64,2048]{2,1,0:T(8,128)(2,1)} %all-to-all-done, s32[1024]{0:T(1024)S(1)} %pad_clamp_fusion.1), kind=kCustom, calls=%fused_computation.clone | custom fusion | bytes 16777344 | tf_op jit(solution)/shard_map/jit(_take)/gather | solution.py:18
  157.5 7.6 %broadcast_select_fusion.1 = bf16[32,64,2048]{2,1,0:T(8,128)(2,1)} fusion(bf16[32,64,2048]{2,1,0:T(8,128)(2,1)} %gather_fusion, pred[32]{0:T(512)(128)(4,1)S(1)} %compare_and_fusion.1), kind=kLoop, calls=%fused_computation.52 | loop fusion | flops 4194304 | bytes 16777248 | tf_op jit(solution)/shard_map/jit(_take)/select_n | solution.py:18
  165.1 138.7 %all-gather.3.cloned.1.call-done = bf16[1,2048,2048]{2,1,0:T(8,128)(2,1)} async-done(((bf16[1,64,2048]{2,1,0:T(8,128)(2,1)}), bf16[1,2048,2048]{2,1,0:T(8,128)(2,1)}) %all-gather.3.cloned.1.call-update) | async-done | bytes 8388624 | tf_op jit(solution)/shard_map/all_gather | solution.py:41
  303.8 8.5 %gather_fusion.1 = bf16[32,64,2048]{2,1,0:T(8,128)(2,1)} fusion(bf16[32,64,2048]{2,1,0:T(8,128)(2,1)} %bitcast.121, s32[1024]{0:T(1024)S(1)} %pad_clamp_fusion), kind=kCustom, calls=%fused_computation.1.clone | custom fusion | bytes 16777344 | tf_op jit(solution)/shard_map/jit(_take)/gather | solution.py:18
  312.3 7.7 %broadcast_select_fusion = bf16[32,64,2048]{2,1,0:T(8,128)(2,1)} fusion(bf16[32,64,2048]{2,1,0:T(8,128)(2,1)} %gather_fusion.1, pred[32]{0:T(512)(128)(4,1)S(1)} %compare_and_fusion), kind=kLoop, calls=%fused_computation.51 | loop fusion | flops 4194304 | bytes 16777248 | tf_op jit(solution)/shard_map/jit(_take)/select_n | solution.py:18
  320.0 1.5 conditional.4
  320.0 1.5 broadcast_in_dim.32
  321.5 1.5 collective-permute-start.1
  322.9 3.4 collective-permute-done.1
  327.6 27.1 %collective-permute-done.2 = bf16[2048,256]{1,0:T(8,128)(2,1)S(1)} collective-permute-done((bf16[2048,256]{1,0:T(8,128)(2,1)}, bf16[2048,256]{1,0:T(8,128)(2,1)S(1)}, u32[]{:S(2)}, u32[]{:S(2)}) %collective-permute-start.2) | collective-permute-done | bytes 1048608 | tf_op jit(solution)/shard_map/ppermute | solution.py:10
  357.1 165.7 %collective-permute-done.3 = bf16[2048,256]{1,0:T(8,128)(2,1)S(1)} collective-permute-done((bf16[2048,256]{1,0:T(8,128)(2,1)}, bf16[2048,256]{1,0:T(8,128)(2,1)S(1)}, u32[]{:S(2)}, u32[]{:S(2)}) %collective-permute-start.3) | collective-permute-done | bytes 1048608 | tf_op jit(solution)/shard_map/ppermute | solution.py:10
  522.8 50.4 %conditional.7 = (bf16[2,2048,256]{2,1,0:T(8,128)(2,1)}) conditional(s32[]{:T(128)} %convert_element_type.204, bf16[2,2048,256]{2,1,0:T(8,128)(2,1)} %get-tuple-element.316, (bf16[2048,256]{1,0:T(8,128)(2,1)S(1)}, bf16[2,2048,256]{2,1,0:T(8,128)(2,1)S(1)}, s32[2]{0:T(128)S(1)}, bf16[2048,2048]{1,0:T(8,128)(2,1)}, ...), branch_computations={%region_20.22_spmd, %region_21.27_spmd} | conditional | flops 4306501632 | bytes 95420856 | solution.py:68
  523.8 2.8 fusion.27
  526.6 10.2 %while.88 = (s32[]{:T(128)}, bf16[2048,256]{1,0:T(8,128)(2,1)S(1)}, f32[2048,256]{1,0:T(8,128)}, s32[]{:T(128)}, bf16[2048,2048]{1,0:T(8,128)(2,1)}, /*index=5*/s32[]{:T(128)}) while((s32[]{:T(128)}, bf16[2048,256]{1,0:T(8,128)(2,1)S(1)}, f32[2048,256]{1,0:T(8,128)}, s32[]{:T(128)}, bf16[2048,2048]{1,0:T(8,128)(2,1)}, ...), condition=%wide.region_23.24_spmd, body=%wide.region_22.23_spmd.sunk | while | flops 2149056512 | bytes 33554556 | solution.py:29
  527.3 1.5 copy-done.18
  528.8 6.0 %convert_add_fusion.24 = (f32[2048,256]{1,0:T(8,128)S(1)}, bf16[2048,256]{1,0:T(8,128)(2,1)S(1)}) fusion(f32[2048,256]{1,0:T(8,128)S(1)} %copy-done.18, bf16[2048,2048]{1,0:T(8,128)(2,1)} %get-tuple-element.751, bf16[2048,256]{1,0:T(8,128)(2,1)S(1)} %copy.109), kind=kOutput, calls=%fused_computation.39.clone.1 | convolution fusion | flops 2149056512 | bytes 14680064 | tf_op jit(solution)/shard_map/cond/branch_1_fun/while/body/dot_general | solution.py:26
  534.8 1.3 copy-done.19
  536.8 3.7 fusion.25
  540.5 29.2 %while.89 = (s32[]{:T(128)}, bf16[2048,256]{1,0:T(8,128)(2,1)S(1)}, f32[2048,256]{1,0:T(8,128)}, s32[]{:T(128)}, bf16[2048,2048]{1,0:T(8,128)(2,1)}, /*index=5*/s32[]{:T(128)}) while((s32[]{:T(128)}, bf16[2048,256]{1,0:T(8,128)(2,1)S(1)}, f32[2048,256]{1,0:T(8,128)}, s32[]{:T(128)}, bf16[2048,2048]{1,0:T(8,128)(2,1)}, ...), condition=%wide.region_25.26_spmd, body=%wide.region_24.25_spmd.sunk | while | flops 2149056512 | bytes 33554556 | solution.py:29
  541.2 1.5 copy-done.10
  542.7 6.0 %convert_add_fusion.25 = (f32[2048,256]{1,0:T(8,128)S(1)}, bf16[2048,256]{1,0:T(8,128)(2,1)S(1)}) fusion(f32[2048,256]{1,0:T(8,128)S(1)} %copy-done.10, bf16[2048,2048]{1,0:T(8,128)(2,1)} %get-tuple-element.769, bf16[2048,256]{1,0:T(8,128)(2,1)S(1)} %copy.110), kind=kOutput, calls=%fused_computation.41.clone.1 | convolution fusion | flops 2149056512 | bytes 14680064 | tf_op jit(solution)/shard_map/cond/branch_1_fun/while/body/dot_general | solution.py:26
  548.7 1.3 copy-done.11
  550.8 1.5 copy-done.10
  552.3 6.0 %convert_add_fusion.25 = (f32[2048,256]{1,0:T(8,128)S(1)}, bf16[2048,256]{1,0:T(8,128)(2,1)S(1)}) fusion(f32[2048,256]{1,0:T(8,128)S(1)} %copy-done.10, bf16[2048,2048]{1,0:T(8,128)(2,1)} %get-tuple-element.769, bf16[2048,256]{1,0:T(8,128)(2,1)S(1)} %copy.110), kind=kOutput, calls=%fused_computation.41.clone.1 | convolution fusion | flops 2149056512 | bytes 14680064 | tf_op jit(solution)/shard_map/cond/branch_1_fun/while/body/dot_general | solution.py:26
  560.3 1.5 copy-done.10
  561.8 6.0 %convert_add_fusion.25 = (f32[2048,256]{1,0:T(8,128)S(1)}, bf16[2048,256]{1,0:T(8,128)(2,1)S(1)}) fusion(f32[2048,256]{1,0:T(8,128)S(1)} %copy-done.10, bf16[2048,2048]{1,0:T(8,128)(2,1)} %get-tuple-element.769, bf16[2048,256]{1,0:T(8,128)(2,1)S(1)} %copy.110), kind=kOutput, calls=%fused_computation.41.clone.1 | convolution fusion | flops 2149056512 | bytes 14680064 | tf_op jit(solution)/shard_map/cond/branch_1_fun/while/body/dot_general | solution.py:26
  569.8 1.9 fusion.11
  571.7 1.5 pad_maximum_fusion.3
  (45 shorter events, 10.2 us)
Async XLA Ops:
  6.5 297.3 %all-gather.3.cloned.1.call-start = ((), (), s32[]{:S(2)}) async-start(), calls=%async_computation.1 | async-start | bytes 8650752 | tf_op jit(solution)/shard_map/all_gather | solution.py:41
  12.7 11.9 %copy-start.29 = (s32[2,32]{1,0:T(2,128)S(1)}, s32[2,32]{1,0:T(2,128)}, u32[]{:S(2)}) copy-start(s32[2,32]{1,0:T(2,128)} %param.33) | copy-start | bytes 772
  12.7 136.3 %all-to-all-start = ((bf16[32,64,2048]{2,1,0:T(8,128)(2,1)}), bf16[32,64,2048]{2,1,0:T(8,128)(2,1)}, u32[]{:S(2)}, u32[]{:S(2)}) async-start(bf16[32,64,2048]{2,1,0:T(8,128)(2,1)} %stack.39), calls=%async_computation | async-start | bytes 16777216 | tf_op jit(solution)/shard_map/all_to_all | solution.py:39
  23.3 296.7 %collective-permute-start = (bf16[2048,256]{1,0:T(8,128)(2,1)}, bf16[2048,256]{1,0:T(8,128)(2,1)S(1)}, u32[]{:S(2)}, u32[]{:S(2)}) collective-permute-start(bf16[2048,256]{1,0:T(8,128)(2,1)} %broadcast_in_dim.37), channel_id=1, source_target_pairs={{32,0},{64,32},{96,64},{33,1},{65,33},{97,65},{34,2},{66,34},{98,6... | collective-permute-start | bytes 3145736 | tf_op jit(solution)/shard_map/ppermute | solution.py:10
  312.3 7.7 %copy-start = (bf16[2,2048,256]{2,1,0:T(8,128)(2,1)S(1)}, bf16[2,2048,256]{2,1,0:T(8,128)(2,1)}, u32[]{:S(2)}) copy-start(bf16[2,2048,256]{2,1,0:T(8,128)(2,1)} %param.30) | copy-start | bytes 6291460
  312.3 7.7 %copy-start.28 = (s32[2]{0:T(128)S(1)}, s32[2]{0:T(128)}, u32[]{:S(2)}) copy-start(s32[2]{0:T(128)} %param.32) | copy-start | bytes 28
  321.5 4.9 collective-permute-start.1
  326.3 28.4 %collective-permute-start.2 = (bf16[2048,256]{1,0:T(8,128)(2,1)}, bf16[2048,256]{1,0:T(8,128)(2,1)S(1)}, u32[]{:S(2)}, u32[]{:S(2)}) collective-permute-start(bf16[2048,256]{1,0:T(8,128)(2,1)} %get-tuple-element.314), channel_id=1, source_target_pairs={{32,0},{64,32},{96,64},{33,1},{65,33},{97,65},{34,2},{66,34},{98,6... | collective-permute-start | bytes 3145736 | tf_op jit(solution)/shard_map/ppermute | solution.py:10
  354.8 1.0 copy-start.27
  355.8 167.0 %collective-permute-start.3 = (bf16[2048,256]{1,0:T(8,128)(2,1)}, bf16[2048,256]{1,0:T(8,128)(2,1)S(1)}, u32[]{:S(2)}, u32[]{:S(2)}) collective-permute-start(bf16[2048,256]{1,0:T(8,128)(2,1)} %copy-done.27), channel_id=1, source_target_pairs={{32,0},{64,32},{96,64},{33,1},{65,33},{97,65},{34,2},{66,34},{98,6... | collective-permute-start | bytes 3145736 | tf_op jit(solution)/shard_map/ppermute | solution.py:10
  522.8 1.0 copy-start.25
  527.2 1.6 copy-start.18
  534.8 1.3 copy-start.19
  541.2 1.6 copy-start.10
  548.7 1.3 copy-start.11
  550.7 1.6 copy-start.10
  558.3 1.3 copy-start.11
  560.2 1.6 copy-start.10
  567.8 1.3 copy-start.11
  569.7 1.9 copy-start.23
Sparse Core Ops, SparseCore 0:
  9.0 294.8 all-gather.2
